TPU v7x, 256 devices: a whole 4x4x8 slice. The times are simulated.
256 devices in a mesh: samp: 4 (over z_hi, core), vert: 64 (over x, z_lo, y).
Axes of the slice: x: 4, y: 4, z: 8 (z_hi: 2, z_lo: 4; z = z_hi * 4 + z_lo), core: 2. Of those that a mesh axis runs over, the one named last changes fastest.
Arguments:
- inputs: bfloat16 [8, 262144, 128], P('samp', 'vert'), may hold values from -6 to 6
- cotangent: bfloat16 [8, 262144, 128], P('samp', 'vert'), may hold values from -6 to 6
- basis: bfloat16 [262144, 1024], P('vert'), may hold values from -0.0234375 to 0.0234375
- mode_weights: bfloat16 [1024, 128, 128], P('vert'), may hold values from -0.5 to 0.5
- w_up: bfloat16 [128, 512], replicated, may hold values from -0.5 to 0.5
- b_up: float32 [512], replicated, may hold values from -4 to 4
- w_down: bfloat16 [512, 128], replicated, may hold values from -0.25 to 0.25
Outputs:
- grad_input: bfloat16 [8, 262144, 128], P('samp', 'vert')
- grad_modes: float32 [1024, 128, 128], P('vert')
- grad_w_up: float32 [128, 512], replicated
- grad_b_up: float32 [512], replicated
- grad_w_down: float32 [512, 128], replicated
All inputs are finite; a program needn't handle non-finite values.
Results may differ from a plain program's by a relative error of at most 0.0055.
Values may be sent and summed in bfloat16 or wider, within the bound.
No kernel may reach another device: no remote copies, remote signals or barrier semaphores. Data moves between devices by JAX's collectives and lax.ppermute only.
A program may use at most 128 MiB of HBM per device.

v0:
```python
import jax
import jax.numpy as jnp
from jax import lax
from jax.sharding import PartitionSpec as P


def gelu_value(pre_act):
    inner = 0.7978845608 * (pre_act + 0.044715 * pre_act * pre_act * pre_act)
    return 0.5 * pre_act * (1.0 + jnp.tanh(inner))


def gelu_slope(pre_act):
    inner = 0.7978845608 * (pre_act + 0.044715 * pre_act * pre_act * pre_act)
    tangent = jnp.tanh(inner)
    return 0.5 * (1.0 + tangent) + 0.5 * pre_act * (1.0 - tangent * tangent) * 0.7978845608 * (
        1.0 + 3.0 * 0.044715 * pre_act * pre_act
    )


def spectral_part(grad_out, mode_weights, basis):
    mixing = mode_weights.astype(jnp.float32)
    grad_coef = jnp.einsum(
        "skd,kcd->skc", grad_out, mixing, precision=lax.Precision.HIGHEST
    ).astype(jnp.bfloat16)
    return jnp.einsum(
        "vk,skc->svc",
        basis,
        lax.all_gather(grad_coef, "vert", axis=1, tiled=True),
        preferred_element_type=jnp.float32,
    )


def pointwise_part(inputs, cotangent, w_up, b_up, w_down):
    samples_here = inputs.shape[0]
    vertices_here = inputs.shape[1]
    channels = inputs.shape[2]
    flat_inputs = inputs.reshape(samples_here * vertices_here, channels)
    flat_cotangent = cotangent.reshape(samples_here * vertices_here, channels)
    pre_act = jnp.dot(flat_inputs, w_up, preferred_element_type=jnp.float32) + b_up
    hidden = gelu_value(pre_act).astype(jnp.bfloat16)
    grad_hidden = jnp.dot(flat_cotangent, w_down.T, preferred_element_type=jnp.float32)
    grad_pre = (grad_hidden * gelu_slope(pre_act)).astype(jnp.bfloat16)
    pointwise = jnp.dot(grad_pre, w_up.T, preferred_element_type=jnp.float32)
    local_up = jnp.dot(flat_inputs.T, grad_pre, preferred_element_type=jnp.float32)
    local_bias = jnp.sum(grad_pre.astype(jnp.float32), axis=0)
    local_down = jnp.dot(hidden.T, flat_cotangent, preferred_element_type=jnp.float32)
    sums = lax.psum((local_up, local_bias, local_down), ("samp", "vert"))
    return (pointwise.reshape(samples_here, vertices_here, channels), sums)


def per_device(inputs, cotangent, basis, mode_weights, w_up, b_up, w_down):
    channels = inputs.shape[2]
    stacked = jnp.concatenate([inputs, cotangent], axis=2)
    projected = jnp.einsum("vk,svc->skc", basis, stacked, preferred_element_type=jnp.float32)
    owned_sums = lax.psum_scatter(projected, "vert", scatter_dimension=1, tiled=True)
    coeffs = owned_sums[:, :, :channels]
    grad_out = owned_sums[:, :, channels:]
    spectral = spectral_part(grad_out, mode_weights, basis)
    pointwise, mlp_grads = pointwise_part(inputs, cotangent, w_up, b_up, w_down)
    local_modes = jnp.einsum("skc,skd->kcd", coeffs, grad_out, precision=lax.Precision.HIGHEST)
    grad_modes = lax.psum(local_modes, "samp")
    grad_input = (spectral + pointwise).astype(jnp.bfloat16)
    grad_w_up, grad_b_up, grad_w_down = mlp_grads
    return (grad_input, grad_modes, grad_w_up, grad_b_up, grad_w_down)


def solution(mesh):
    in_specs = (
        P("samp", "vert", None),
        P("samp", "vert", None),
        P("vert", None),
        P("vert", None, None),
        P(),
        P(),
        P(),
    )
    out_specs = (P("samp", "vert", None), P("vert", None, None), P(), P(), P())
    return jax.shard_map(
        per_device, mesh=mesh, in_specs=in_specs, out_specs=out_specs, check_vma=False
    )
```

profile of v0, /device:TPU:0, one launch (start us, length us, event | category | flops | bytes accessed | tf_op | source)
XLA Modules:
  0.0 1230.6 jit_solution(3378659776492930055)
XLA Ops:
  7.2 0.0 copy-start
  7.2 0.0 all-reduce.10.cloned.1.call-start
  7.2 0.0 copy-start.2
  7.2 4.1 fusion.42
  11.3 0.0 copy-start.5
  11.4 7.7 fusion.11
  19.1 15.0 %convert_reduce_fusion = (f32[512]{0:T(512)S(1)}, bf16[8192,512]{1,0:T(8,128)(2,1)}) fusion(f32[8192,512]{1,0:T(8,128)S(1)} %fusion.42, f32[512]{0:T(512)S(1)} %copy-done.6, bf16[8192,128]{1,0:T(8,128)(2,1)} %bitcast.42, bf16[512,128]{1,0:T(8,128)(2,1)S(1)} %copy-done.5), kind=kOutput, calls=%fused_computation.10 | convolution fusion | flops 1166016000 | bytes 27398144 | tf_op jit(solution)/shard_map/dot_general | solution.py:41
  34.1 6.4 convolution_bitcast_fusion
  40.5 0.0 all-reduce.10.cloned.1.call-update
  40.6 0.2 all-reduce.8.cloned.1.call-start
  40.8 2.8 copy.32
  43.6 4.1 copy.33
  47.7 8.2 fusion.24
  55.9 2.3 copy.34
  58.2 0.0 all-reduce.8.cloned.1.call-update
  58.2 0.0 all-reduce.6.cloned.1.call-start
  58.3 7.7 fusion.43
  66.0 5.7 copy.36
  71.7 0.0 copy-done.7
  71.7 0.6 dynamic-slice
  72.9 79.6 %psum.30 = f32[512]{0:T(512)} all-reduce(f32[512]{0:T(512)S(1)} %get-tuple-element.27), channel_id=1, replica_groups=mesh['samp'=4,'vert'=64] {'samp','vert'}, use_global_device_ids=true, to_apply=%region_4.0 | all-reduce | flops 512 | bytes 4096 | tf_op jit(solution)/shard_map/psum | solution.py:47
  152.5 142.1 %all-reduce.10.cloned.1.call-done = (f32[128,512]{0,1:T(8,128)}, f32[512,128]{1,0:T(8,128)}) async-done(((f32[128,512]{0,1:T(8,128)}, f32[512,128]{1,0:T(8,128)}), (f32[128,512]{0,1:T(8,128)}, f32[512,128]{1,0:T(8,128)})) %all-reduce.10.cloned.1.call-update) | async-done | bytes 524304 | tf_op jit(solution)/shard_map/psum | solution.py:47
  294.5 1.8 copy.38
  296.3 717.1 %all-reduce.8.cloned.1.call-done = f32[2,1024,256]{2,0,1:T(2,128)} async-done(((f32[2,1024,256]{2,0,1:T(2,128)}), f32[2,1024,256]{2,0,1:T(2,128)}) %all-reduce.8.cloned.1.call-update) | async-done | bytes 2097168
  1013.5 3.5 fusion.31
  1017.0 0.0 all-reduce.6.cloned.1.call-update
  1017.0 1.7 fusion.29
  1018.7 192.9 %all_gather.3 = bf16[2,1024,128]{2,0,1:T(2,128)(2,1)S(1)} all-gather(bf16[2,16,128]{2,0,1:T(2,128)(2,1)S(1)} %fusion.29), channel_id=1, replica_groups=mesh['samp'=4,'vert'=64] {'vert'}, dimensions={1}, use_global_device_ids=true | all-gather | bytes 532480 | tf_op jit(solution)/shard_map/all_gather | solution.py:28
  1211.6 7.0 fusion.18
  1218.6 2.5 copy.37
  1221.1 2.3 copy.45
  1223.4 0.7 copy.46
  (13 shorter events, 0.0 us)
Async XLA Ops:
  7.2 1009.9 %copy-start = (bf16[16,128,128]{2,1,0:T(8,128)(2,1)S(1)}, bf16[16,128,128]{2,1,0:T(8,128)(2,1)}, u32[]{:S(2)}) copy-start(bf16[16,128,128]{2,1,0:T(8,128)(2,1)} %param.10) | copy-start | bytes 1572868
  7.2 287.4 %all-reduce.10.cloned.1.call-start = ((), (), s32[]{:S(2)}) async-start(), calls=%async_computation.2 | async-start | bytes 1048576 | tf_op jit(solution)/shard_map/psum | solution.py:47
  7.2 4.1 copy-start.2
  7.2 4.1 copy-start.6
  11.3 7.7 copy-start.5
  19.1 15.0 %copy-start.1 = (bf16[2,4096,128]{2,1,0:T(8,128)(2,1)S(1)}, bf16[2,4096,128]{2,1,0:T(8,128)(2,1)}, u32[]{:S(2)}) copy-start(bf16[2,4096,128]{2,1,0:T(8,128)(2,1)} %param.7) | copy-start | bytes 6291460
  40.6 972.9 %all-reduce.8.cloned.1.call-start = ((), (), s32[]{:S(2)}) async-start(), calls=%async_computation.1 | async-start | bytes 4194304
  47.7 10.6 copy-start.3
  58.2 1162.9 %all-reduce.6.cloned.1.call-start = ((), (), s32[]{:S(2)}) async-start(), calls=%async_computation | async-start | bytes 2097152 | tf_op jit(solution)/shard_map/psum | solution.py:61
  66.0 5.7 copy-start.7
  1211.6 11.8 copy-start.4
Sparse Core Ops, SparseCore 0:
  40.7 253.8 all-reduce.9
  297.7 715.6 all-reduce.7
  1017.1 68.9 all-reduce.5
where the time goes:
time: 1230 us
  waiting for transfers between devices  859 us (70%)
  blocking collectives  272 us (22%)
  matrix products  61.4 us (5%)
  local copies, waits for them, and re-layouts  22.7 us (2%)
  between operations  14.5 us (1%)
    unnamed x4, waiting for transfers between devices  717 us
    all_gather x1, blocking collectives, spectral_part(): lax.all_gather(grad_coef, 'vert', axis=1, tiled=True)  193 us
    psum x1, waiting for transfers between devices, pointwise_part(): sums = lax.psum((local_up, local_bias, local_down), ('samp', 'vert'))  142 us
    psum x1, blocking collectives, pointwise_part(): sums = lax.psum((local_up, local_bias, local_down), ('samp', 'vert'))  79.6 us
  transfers between devices with their start and end apart: 3, of which 2 were waited for; matrix products, arithmetic and copies ran while one was open for 4% of the time, Pallas kernels for 0%

commit v1 on v0

--- a/solution.py
+++ b/solution.py
@@ -44,7 +44,7 @@
     local_up = jnp.dot(flat_inputs.T, grad_pre, preferred_element_type=jnp.float32)
     local_bias = jnp.sum(grad_pre.astype(jnp.float32), axis=0)
     local_down = jnp.dot(hidden.T, flat_cotangent, preferred_element_type=jnp.float32)
-    sums = lax.psum((local_up, local_bias, local_down), ("samp", "vert"))
+    sums = lax.psum(lax.psum((local_up, local_bias, local_down), "samp"), "vert")
     return (pointwise.reshape(samples_here, vertices_here, channels), sums)
 
 

time: 1230 us -> 1040 us (0.85)
  waiting for transfers between devices: 859 us -> 549 us
  blocking collectives: 272 us -> 390 us
    unnamed x4, waiting for transfers between devices: 717 us -> 508 us
    psum x1 -> x2, blocking collectives: 79.6 us -> 199 us  [the longest x1 187 us: pointwise_part(): lax.psum(lax.psum((local_up, local_bias, local_down), 'samp'), 'vert')]
    psum x1, waiting for transfers between devices: 142 us -> 41.7 us  [pointwise_part(): lax.psum((local_up, local_bias, local_down), 'samp')]
where the time goes in v1:
time: 1040 us
  waiting for transfers between devices  549 us (53%)
  blocking collectives  390 us (38%)
  matrix products  61.4 us (6%)
  local copies, waits for them, and re-layouts  21.8 us (2%)
  between operations  14.5 us (1%)
    unnamed x4, waiting for transfers between devices  508 us
    all_gather x1, blocking collectives, spectral_part(): lax.all_gather(grad_coef, 'vert', axis=1, tiled=True)  191 us
    psum x1, blocking collectives, pointwise_part(): lax.psum(lax.psum((local_up, local_bias, local_down), 'samp'), 'vert')  187 us
    psum x1, waiting for transfers between devices, pointwise_part(): lax.psum((local_up, local_bias, local_down), 'samp')  41.7 us
  transfers between devices with their start and end apart: 3, of which 2 were waited for; matrix products, arithmetic and copies ran while one was open for 4% of the time, Pallas kernels for 0%

profile of v1, /device:TPU:0, one launch (start us, length us, event | category | flops | bytes accessed | tf_op | source)
XLA Modules:
  0.0 1037.1 jit_solution(10023099710026586386)
XLA Ops:
  7.2 0.0 copy-start
  7.2 0.0 all-reduce.11.cloned.1.call-start
  7.2 0.0 copy-start.2
  7.2 4.1 fusion.42
  11.3 0.0 copy-start.6
  11.4 7.7 fusion.11
  19.1 15.0 %convert_reduce_fusion = (f32[512]{0:T(512)S(1)}, bf16[8192,512]{1,0:T(8,128)(2,1)}) fusion(f32[8192,512]{1,0:T(8,128)S(1)} %fusion.42, f32[512]{0:T(512)S(1)} %copy-done.7, bf16[8192,128]{1,0:T(8,128)(2,1)} %bitcast.42, bf16[512,128]{1,0:T(8,128)(2,1)S(1)} %copy-done.6), kind=kOutput, calls=%fused_computation.10 | convolution fusion | flops 1166016000 | bytes 27398144 | tf_op jit(solution)/shard_map/dot_general | solution.py:41
  34.1 6.4 convolution_bitcast_fusion
  40.5 0.0 all-reduce.11.cloned.1.call-update
  40.6 0.2 all-reduce.9.cloned.1.call-start
  40.8 2.8 copy.32
  43.6 4.1 copy.33
  47.7 8.2 fusion.24
  55.9 2.3 copy.34
  58.2 41.7 %all-reduce.11.cloned.1.call-done = (f32[128,512]{0,1:T(8,128)}, f32[512,128]{1,0:T(8,128)}) async-done(((f32[128,512]{0,1:T(8,128)}, f32[512,128]{1,0:T(8,128)}), (f32[128,512]{0,1:T(8,128)}, f32[512,128]{1,0:T(8,128)})) %all-reduce.11.cloned.1.call-update) | async-done | bytes 524304 | tf_op jit(solution)/shard_map/psum | solution.py:47
  99.9 0.0 all-reduce.9.cloned.1.call-update
  99.9 0.0 all-reduce.7.cloned.1.call-start
  100.0 7.7 fusion.43
  107.7 5.6 copy.36
  113.3 0.6 dynamic-slice
  114.6 12.1 %psum.52 = f32[512]{0:T(512)S(1)} all-reduce(f32[512]{0:T(512)S(1)} %get-tuple-element.30), channel_id=1, replica_groups=mesh['samp'=4,'vert'=64] {'samp'}, use_global_device_ids=true, to_apply=%region_5.0 | all-reduce | flops 512 | bytes 4096 | tf_op jit(solution)/shard_map/psum | solution.py:47
  126.7 187.0 %psum.53 = f32[512]{0:T(512)} all-reduce(f32[512]{0:T(512)S(1)} %psum.52), channel_id=1, replica_groups=mesh['samp'=4,'vert'=64] {'vert'}, use_global_device_ids=true, to_apply=%region_6.0 | all-reduce | flops 512 | bytes 4096 | tf_op jit(solution)/shard_map/psum | solution.py:47
  313.7 507.6 %all-reduce.9.cloned.1.call-done = (f32[2,1024,256]{2,0,1:T(2,128)}, f32[128,512]{0,1:T(8,128)}, f32[512,128]{1,0:T(8,128)}) async-done(((f32[2,1024,256]{2,0,1:T(2,128)}, f32[128,512]{0,1:T(8,128)}, f32[512,128]{1,0:T(8,128)}), (f32[2,1024,256]{2,0,1:T(2,128)}, f32[128,512]{0,1:T(8,128)}, f32[512,128]{1,0:T(8,128)})) %all-reduce.9.cloned.1.call-update) | async-done | bytes 2621456
  821.3 3.5 fusion.31
  824.8 1.7 fusion.29
  826.5 0.0 all-reduce.7.cloned.1.call-update
  826.5 190.7 %all_gather.3 = bf16[2,1024,128]{2,0,1:T(2,128)(2,1)S(1)} all-gather(bf16[2,16,128]{2,0,1:T(2,128)(2,1)S(1)} %fusion.29), channel_id=1, replica_groups=mesh['samp'=4,'vert'=64] {'vert'}, dimensions={1}, use_global_device_ids=true | all-gather | bytes 532480 | tf_op jit(solution)/shard_map/all_gather | solution.py:28
  1017.2 7.0 fusion.18
  1024.3 2.5 copy.37
  1026.7 0.8 copy.38
  1027.6 2.3 copy.47
  1029.9 0.7 copy.48
  (16 shorter events, 0.0 us)
Async XLA Ops:
  7.2 817.7 %copy-start = (bf16[16,128,128]{2,1,0:T(8,128)(2,1)S(1)}, bf16[16,128,128]{2,1,0:T(8,128)(2,1)}, u32[]{:S(2)}) copy-start(bf16[16,128,128]{2,1,0:T(8,128)(2,1)} %param.10) | copy-start | bytes 1572868
  7.2 92.7 %all-reduce.11.cloned.1.call-start = ((), (), s32[]{:S(2)}) async-start(), calls=%async_computation.2 | async-start | bytes 1048576 | tf_op jit(solution)/shard_map/psum | solution.py:47
  7.2 4.1 copy-start.2
  7.2 4.1 copy-start.7
  11.3 7.7 copy-start.6
  19.1 15.0 %copy-start.1 = (bf16[2,4096,128]{2,1,0:T(8,128)(2,1)S(1)}, bf16[2,4096,128]{2,1,0:T(8,128)(2,1)}, u32[]{:S(2)}) copy-start(bf16[2,4096,128]{2,1,0:T(8,128)(2,1)} %param.7) | copy-start | bytes 6291460
  40.6 780.7 %all-reduce.9.cloned.1.call-start = ((), (), s32[]{:S(2)}) async-start(), calls=%async_computation.1 | async-start | bytes 5242880
  47.7 52.3 %copy-start.3 = (bf16[128,512]{1,0:T(8,128)(2,1)S(1)}, bf16[128,512]{1,0:T(8,128)(2,1)}, u32[]{:S(2)}) copy-start(bf16[128,512]{1,0:T(8,128)(2,1)} %param.11) | copy-start | bytes 393220
  99.9 927.6 %all-reduce.7.cloned.1.call-start = ((), (), s32[]{:S(2)}) async-start(), calls=%async_computation | async-start | bytes 2097152 | tf_op jit(solution)/shard_map/psum | solution.py:61
  107.7 5.6 copy-start.8
  1017.2 9.5 copy-start.5
  1017.2 12.6 %copy-start.4 = (f32[512,128]{1,0:T(8,128)S(1)}, f32[512,128]{1,0:T(8,128)}, u32[]{:S(2)}) copy-start(f32[512,128]{1,0:T(8,128)} %get-tuple-element.36) | copy-start | bytes 786436
Sparse Core Ops, SparseCore 0:
  40.7 59.1 all-reduce.10
  103.3 717.9 all-reduce.8
  826.7 69.1 all-reduce.6

commit v2 on v0

--- a/solution.py
+++ b/solution.py
@@ -25,7 +25,9 @@
     return jnp.einsum(
         "vk,skc->svc",
         basis,
-        lax.all_gather(grad_coef, "vert", axis=1, tiled=True),
+        jnp.concatenate(
+            lax.all_to_all(jnp.stack([grad_coef] * lax.axis_size("vert")), "vert", 0, 0), axis=1
+        ),
         preferred_element_type=jnp.float32,
     )
 

time: 1230 us -> 1110 us (0.902)
  blocking collectives: 272 us -> 77.1 us
  waiting for transfers between devices: 859 us -> 902 us
    all_gather x1 -> x0, blocking collectives: 193 us -> none  [spectral_part(): lax.all_gather(grad_coef, 'vert', axis=1, tiled=True)]
    psum x1, waiting for transfers between devices: 0.01 us -> 61.3 us  [per_device(): grad_modes = lax.psum(local_modes, 'samp')]
    unnamed x4, waiting for transfers between devices: 717 us -> 683 us
    psum x1, waiting for transfers between devices: 142 us -> 158 us  [pointwise_part(): sums = lax.psum((local_up, local_bias, local_down), ('samp', 'vert'))]
  transfers between devices with their start and end apart: 3 -> 4, of which waited for: 2 -> 3; matrix products, arithmetic and copies ran while one was open for 4% -> 6% of each run, Pallas kernels for 0% -> 0%
where the time goes in v2:
time: 1110 us; the launch traced here: 1100 us
  waiting for transfers between devices  902 us (81%)
  blocking collectives  77.1 us (7%)
  matrix products  70.6 us (6%)
  local copies, waits for them, and re-layouts  26.8 us (2%)
  between operations  16.3 us (1%)
    unnamed x4, waiting for transfers between devices  683 us
    psum x1, waiting for transfers between devices, pointwise_part(): sums = lax.psum((local_up, local_bias, local_down), ('samp', 'vert'))  158 us
    psum x1, blocking collectives, pointwise_part(): sums = lax.psum((local_up, local_bias, local_down), ('samp', 'vert'))  77.1 us
    psum x1, waiting for transfers between devices, per_device(): grad_modes = lax.psum(local_modes, 'samp')  61.3 us
  transfers between devices with their start and end apart: 4, of which 3 were waited for; matrix products, arithmetic and copies ran while one was open for 6% of the time, Pallas kernels for 0%

profile of v2, /device:TPU:0, one launch (start us, length us, event | category | flops | bytes accessed | tf_op | source)
XLA Modules:
  0.0 1103.0 jit_solution(9852572421213501928)
XLA Ops:
  8.0 0.0 copy-start
  8.0 0.0 all-reduce.8.cloned.1.call-start
  8.1 4.2 copy.30
  12.2 4.1 copy.31
  16.3 10.6 fusion.24
  26.9 4.1 copy.32
  31.0 0.0 all-reduce.8.cloned.1.call-update
  31.1 0.0 copy-start.7
  31.1 8.1 fusion.41
  39.2 0.6 dynamic-slice
  40.4 17.4 %convert_reduce_fusion = (f32[512]{0:T(512)S(1)}, bf16[8192,512]{1,0:T(8,128)(2,1)}) fusion(f32[8192,512]{1,0:T(8,128)} %fusion.41, f32[512]{0:T(512)S(1)} %copy-done.6, bf16[8192,128]{1,0:T(8,128)(2,1)} %bitcast.46, bf16[512,128]{1,0:T(8,128)(2,1)S(1)} %copy-done.5), kind=kOutput, calls=%fused_computation.10 | convolution fusion | flops 1166016000 | bytes 27398144 | tf_op jit(solution)/shard_map/dot_general | solution.py:43
  57.8 8.2 fusion.11
  66.0 682.6 %all-reduce.8.cloned.1.call-done = f32[2,1024,256]{2,0,1:T(2,128)} async-done(((f32[2,1024,256]{2,0,1:T(2,128)}), f32[2,1024,256]{2,0,1:T(2,128)}) %all-reduce.8.cloned.1.call-update) | async-done | bytes 2097168
  748.6 1.7 fusion.29
  750.3 0.9 stack.2
  751.1 9.6 all-to-all-start
  760.8 0.0 all-reduce.10.cloned.1.call-start
  760.8 6.4 convolution_bitcast_fusion
  767.3 0.0 all-reduce.10.cloned.1.call-update
  767.3 0.3 all-reduce.6.cloned.1.call-start
  767.6 3.6 fusion.30
  771.1 0.0 all-reduce.6.cloned.1.call-update
  771.2 7.7 fusion.42
  778.8 5.7 copy.36
  784.5 77.1 %psum.30 = f32[512]{0:T(512)} all-reduce(f32[512]{0:T(512)S(1)} %get-tuple-element.22), channel_id=1, replica_groups=mesh['samp'=4,'vert'=64] {'samp','vert'}, use_global_device_ids=true, to_apply=%region_4.0 | all-reduce | flops 512 | bytes 4096 | tf_op jit(solution)/shard_map/psum | solution.py:49
  861.6 158.3 %all-reduce.10.cloned.1.call-done = (f32[128,512]{0,1:T(8,128)}, f32[512,128]{1,0:T(8,128)}) async-done(((f32[128,512]{0,1:T(8,128)}, f32[512,128]{1,0:T(8,128)}), (f32[128,512]{0,1:T(8,128)}, f32[512,128]{1,0:T(8,128)})) %all-reduce.10.cloned.1.call-update) | async-done | bytes 524304 | tf_op jit(solution)/shard_map/psum | solution.py:49
  1019.9 1.8 copy.38
  1021.7 7.1 fusion.18
  1028.8 2.5 copy.37
  1031.3 61.3 %all-reduce.6.cloned.1.call-done = f32[16,128,128]{2,1,0:T(8,128)} async-done(((f32[16,128,128]{2,1,0:T(8,128)}), f32[16,128,128]{2,1,0:T(8,128)}) %all-reduce.6.cloned.1.call-update) | async-done | bytes 1048592 | tf_op jit(solution)/shard_map/psum | solution.py:63
  1092.6 2.3 copy.44
  1094.9 0.7 copy.45
  (17 shorter events, 0.1 us)
Async XLA Ops:
  8.0 740.6 %copy-start = (bf16[16,128,128]{2,1,0:T(8,128)(2,1)S(1)}, bf16[16,128,128]{2,1,0:T(8,128)(2,1)}, u32[]{:S(2)}) copy-start(bf16[16,128,128]{2,1,0:T(8,128)(2,1)} %param.10) | copy-start | bytes 1572868
  8.0 740.6 %all-reduce.8.cloned.1.call-start = ((), (), s32[]{:S(2)}) async-start(), calls=%async_computation.2 | async-start | bytes 4194304
  16.3 14.7 %copy-start.2 = (bf16[2,4096,128]{2,1,0:T(8,128)(2,1)S(1)}, bf16[2,4096,128]{2,1,0:T(8,128)(2,1)}, u32[]{:S(2)}) copy-start(bf16[2,4096,128]{2,1,0:T(8,128)(2,1)} %param.7) | copy-start | bytes 6291460
  16.3 14.7 %copy-start.3 = (bf16[128,512]{1,0:T(8,128)(2,1)S(1)}, bf16[128,512]{1,0:T(8,128)(2,1)}, u32[]{:S(2)}) copy-start(bf16[128,512]{1,0:T(8,128)(2,1)} %param.11) | copy-start | bytes 393220
  31.1 8.1 copy-start.7
  31.1 9.3 copy-start.5
  31.1 9.3 copy-start.6
  40.4 17.4 %copy-start.1 = (f32[8192,512]{1,0:T(8,128)S(1)}, f32[8192,512]{1,0:T(8,128)}, u32[]{:S(2)}) copy-start(f32[8192,512]{1,0:T(8,128)} %fusion.41) | copy-start | bytes 50331652
  751.1 270.5 %all-to-all-start = ((bf16[64,2,16,128]{3,2,1,0:T(8,128)(2,1)}), bf16[64,2,16,128]{3,2,1,0:T(8,128)(2,1)S(1)}, u32[]{:S(2)}, u32[]{:S(2)}) async-start(bf16[64,2,16,128]{3,2,1,0:T(8,128)(2,1)} %stack.2), calls=%async_computation | async-start | bytes 1048576 | tf_op jit(solution)/shard_map/all_to_all | solution.py:29
  760.8 259.1 %all-reduce.10.cloned.1.call-start = ((), (), s32[]{:S(2)}) async-start(), calls=%async_computation.3 | async-start | bytes 1048576 | tf_op jit(solution)/shard_map/psum | solution.py:49
  767.3 325.3 %all-reduce.6.cloned.1.call-start = ((), (), s32[]{:S(2)}) async-start(), calls=%async_computation.1 | async-start | bytes 2097152 | tf_op jit(solution)/shard_map/psum | solution.py:63
  1021.7 73.2 %copy-start.4 = (f32[512,128]{1,0:T(8,128)S(1)}, f32[512,128]{1,0:T(8,128)}, u32[]{:S(2)}) copy-start(f32[512,128]{1,0:T(8,128)} %get-tuple-element.28) | copy-start | bytes 786436
Sparse Core Ops, SparseCore 0:
  31.2 717.3 all-reduce.7
Sparse Core Ops, SparseCore 1:
  768.4 251.4 all-reduce.9
  1023.2 69.4 all-reduce.5
